TPU v7x, 256 devices: a whole 4x4x8 slice. The times are simulated.
256 devices in a mesh: snap: 16 (over z, y_lo), space: 16 (over x, y_hi, core).
Axes of the slice: x: 4, y: 4 (y_hi: 2, y_lo: 2; y = y_hi * 2 + y_lo), z: 8, core: 2. Of those that a mesh axis runs over, the one named last changes fastest.
Arguments:
- snapshots: bfloat16 [2048, 2, 64, 720], P('snap', None, 'space'), may hold values from -6 to 6
- lon_coeff: float32 [2, 64, 720], P(None, 'space'), may hold values from 0.05 to 0.24
- lat_coeff: float32 [2, 64, 720], P(None, 'space'), may hold values from 0.1 to 0.24
Outputs:
- gram: float32 [2048, 2048], P('snap', 'space')
All inputs are finite; a program needn't handle non-finite values.
Results may differ from a plain program's by a relative error of at most 0.00062.
Values may be sent and summed in bfloat16 or wider, within the bound.
A program may use at most 128 MiB of HBM per device.

v0:
```python
import math
import jax
import jax.numpy as jnp
from jax import lax
from jax.sharding import PartitionSpec as P


def padded_2(cells, sides, width):
    for axis, dim in sides:
        count = lax.axis_size(axis)
        ends = count - 1
        head = lax.slice_in_dim(cells, 0, width, axis=dim)
        tail = lax.slice_in_dim(cells, cells.shape[dim] - width, cells.shape[dim], axis=dim)
        cells = jnp.concatenate(
            [
                lax.ppermute(tail, axis, [(i, (i + 1) % count) for i in range(ends)]),
                cells,
                lax.ppermute(head, axis, [((i + 1) % count, i) for i in range(ends)]),
            ],
            axis=dim,
        )
    return cells


def inner_tile(left, right):
    return lax.dot_general(
        left, right, (((1,), (1,)), ((), ())), preferred_element_type=jnp.float32
    )


def shards(snapshots, lon_coeff, lat_coeff):
    snap_rows, fields, rows, nlon = snapshots.shape
    bands = lax.axis_size("space")
    padded = padded_2(snapshots, (("space", 2),), 1).astype(jnp.float32)
    values = snapshots.astype(jnp.float32)
    lon_part = jnp.roll(values, 1, axis=3) + jnp.roll(values, -1, axis=3) - 2.0 * values
    lat_part = padded[:, :, 2:] + padded[:, :, :-2] - 2.0 * values
    smooth = values + lon_coeff * lon_part + lat_coeff * lat_part
    nlat = bands * rows
    every_row = jnp.arange(nlat).astype(jnp.float32)
    every_cos = jnp.cos((45.0 + 0.5 * (every_row + 0.5 - nlat / 2.0)) * (math.pi / 180.0))
    total = fields * nlon * jnp.sum(every_cos)
    my_rows = (lax.axis_index("space") * rows + jnp.arange(rows)).astype(jnp.float32)
    cosine = jnp.cos((45.0 + 0.5 * (my_rows + 0.5 - nlat / 2.0)) * (math.pi / 180.0))
    factor = jnp.sqrt(cosine) * total ** (-0.25)
    scaled = (smooth * factor[:, None]).astype(jnp.bfloat16).reshape(snap_rows, -1)
    partial_value = inner_tile(scaled, lax.all_gather(scaled, "snap", axis=0, tiled=True))
    return lax.psum_scatter(partial_value, "space", scatter_dimension=1, tiled=True)


def solution(mesh):
    return jax.shard_map(
        shards,
        mesh=mesh,
        in_specs=(P("snap", None, "space", None), P(None, "space", None), P(None, "space", None)),
        out_specs=P("snap", "space"),
        check_vma=False,
    )
```

profile of v0, /device:TPU:2, one launch (start us, length us, event | category | flops | bytes accessed | tf_op | source)
XLA Modules:
  0.0 613.8 jit_solution(12110628258936550416)
XLA Ops:
  6.5 0.0 copy-start
  6.5 0.0 all-gather.2.cloned.1.call-start
  6.5 1.3 fusion.10
  7.8 1.9 collective-permute-start
  9.7 6.0 collective-permute-start.1
  15.8 0.6 cosine_reduce_fusion
  16.4 0.7 fusion.9
  17.9 0.1 sqrt_multiply_fusion
  17.9 0.0 copy-done
  17.9 0.4 fusion.8
  18.3 0.0 copy-start.1
  18.3 0.0 copy-start.2
  18.4 0.7 collective-permute-done
  19.0 1.8 collective-permute-done.1
  20.8 0.3 maximum_convert_fusion
  21.1 0.0 copy-done.1
  21.1 0.0 copy-done.2
  21.2 3.9 fusion.4
  25.1 0.0 all-gather.2.cloned.1.call-update
  25.1 0.0 reduce-scatter.2.cloned.1.call-start
  25.1 493.8 %all-gather.2.cloned.1.call-done = bf16[2048,5760]{0,1:T(8,128)(2,1)} async-done(((bf16[128,5760]{0,1:T(8,128)(2,1)}), bf16[2048,5760]{0,1:T(8,128)(2,1)}) %all-gather.2.cloned.1.call-update) | async-done | bytes 23592976 | tf_op jit(solution)/shard_map/all_gather | solution.py:47
  518.9 12.5 %fusion.11 = f32[128,2048]{1,0:T(8,128)} fusion(bf16[128,5760]{0,1:T(8,128)(2,1)} %bitcast.4, bf16[2048,5760]{0,1:T(8,128)(2,1)} %all-gather.2.cloned.1.call-done), kind=kOutput, calls=%fused_computation.16 | convolution fusion | flops 3019898880 | bytes 26116096 | tf_op jit(solution)/shard_map/dot_general | solution.py:26
  531.4 0.0 reduce-scatter.2.cloned.1.call-update
  531.5 75.5 %reduce-scatter.2.cloned.1.call-done = f32[128,128]{1,0:T(8,128)} async-done(((f32[128,2048]{1,0:T(8,128)}), f32[128,128]{1,0:T(8,128)}) %reduce-scatter.2.cloned.1.call-update) | async-done | bytes 65552 | tf_op jit(solution)/shard_map/reduce_scatter | solution.py:48
Async XLA Ops:
  6.5 11.4 %copy-start = (bf16[128,2,4,720]{0,3,2,1:T(8,128)(2,1)S(1)}, bf16[128,2,4,720]{0,3,2,1:T(8,128)(2,1)}, u32[]{:S(2)}) copy-start(bf16[128,2,4,720]{0,3,2,1:T(8,128)(2,1)} %param.3) | copy-start | bytes 4423684
  6.5 512.4 %all-gather.2.cloned.1.call-start = ((), (), s32[]{:S(2)}) async-start(), calls=%async_computation.1 | async-start | bytes 25067520 | tf_op jit(solution)/shard_map/all_gather | solution.py:47
  7.8 11.2 %collective-permute-start = (bf16[128,2,1,720]{0,3,2,1:T(8,128)(2,1)S(1)}, bf16[128,2,1,720]{0,3,2,1:T(8,128)(2,1)S(1)}, u32[]{:S(2)}, u32[]{:S(2)}) collective-permute-start(bf16[128,2,1,720]{0,3,2,1:T(8,128)(2,1)S(1)} %get-tuple-element.9), channel_id=1, source_target_pairs={{0,1},{1,2},{2,3},{3,4},{4,5},{5,6},{6,7},{7,8},{8,9},{9,10},{10,1... | collective-permute-start | bytes 1105928 | tf_op jit(solution)/shard_map/ppermute | solution.py:16
  9.7 11.1 %collective-permute-start.1 = (bf16[128,2,1,720]{0,3,2,1:T(8,128)(2,1)S(1)}, bf16[128,2,1,720]{0,3,2,1:T(8,128)(2,1)S(1)}, u32[]{:S(2)}, u32[]{:S(2)}) collective-permute-start(bf16[128,2,1,720]{0,3,2,1:T(8,128)(2,1)S(1)} %get-tuple-element.10), channel_id=1, source_target_pairs={{1,0},{2,1},{3,2},{4,3},{5,4},{6,5},{7,6},{8,7},{9,8},{10,9},{11,1... | collective-permute-start | bytes 1105928 | tf_op jit(solution)/shard_map/ppermute | solution.py:18
  18.3 2.8 copy-start.1
  18.3 2.8 copy-start.2
  25.1 581.8 %reduce-scatter.2.cloned.1.call-start = ((), (), s32[]{:S(2)}) async-start(), calls=%async_computation.2 | async-start | bytes 1114112 | tf_op jit(solution)/shard_map/reduce_scatter | solution.py:48
Sparse Core Ops, SparseCore 0:
  25.2 493.6 all-gather.1
  531.6 75.2 reduce-scatter.1
where the time goes:
time: 614 us
  waiting for transfers between devices  572 us (93%)
  between operations  14.2 us (2%)
  matrix products  12.5 us (2%)
  starting transfers between devices  8.01 us (1%)
    all_gather x1, waiting for transfers between devices, shards(): lax.all_gather(scaled, 'snap', axis=0, tiled=True)  494 us
    reduce_scatter x1, waiting for transfers between devices, shards(): lax.psum_scatter(partial_value, 'space', scatter_dimension=1, tiled=True)  75.5 us
    dot_general x1, matrix products, inner_tile(): lax.dot_general(left, right, (((1,), (1,)), ((), ())), preferred_element_...  12.5 us
  transfers between devices with their start and end apart: 4, of which 4 were waited for; matrix products, arithmetic and copies ran while one was open for 0% of the time, Pallas kernels for 0%

commit v1 on v0

--- a/solution.py
+++ b/solution.py
@@ -44,7 +44,12 @@
     cosine = jnp.cos((45.0 + 0.5 * (my_rows + 0.5 - nlat / 2.0)) * (math.pi / 180.0))
     factor = jnp.sqrt(cosine) * total ** (-0.25)
     scaled = (smooth * factor[:, None]).astype(jnp.bfloat16).reshape(snap_rows, -1)
-    partial_value = inner_tile(scaled, lax.all_gather(scaled, "snap", axis=0, tiled=True))
+    partial_value = inner_tile(
+        scaled,
+        jnp.concatenate(
+            lax.all_to_all(jnp.stack([scaled] * lax.axis_size("snap")), "snap", 0, 0), axis=0
+        ),
+    )
     return lax.psum_scatter(partial_value, "space", scatter_dimension=1, tiled=True)
 
 

time: 614 us -> 642 us (1.046)
  blocking collectives: 0 us -> 521 us
  waiting for transfers between devices: 572 us -> 74.4 us
    all_to_all x0 -> x1, blocking collectives: none -> 521 us  [shards(): lax.all_to_all(jnp.stack([scaled] * lax.axis_size('snap')), 'snap', 0, 0)]
    all_gather x1 -> x0, waiting for transfers between devices: 494 us -> none  [shards(): lax.all_gather(scaled, 'snap', axis=0, tiled=True)]
  transfers between devices with their start and end apart: 4 -> 3, of which waited for: 4 -> 3; matrix products, arithmetic and copies ran while one was open for 0% -> 0% of each run, Pallas kernels for 0% -> 0%
where the time goes in v1:
time: 642 us
  blocking collectives  521 us (81%)
  waiting for transfers between devices  74.4 us (12%)
  between operations  14.2 us (2%)
  matrix products  13.5 us (2%)
  starting transfers between devices  7.97 us (1%)
  local copies, waits for them, and re-layouts  6.43 us (1%)
    all_to_all x1, blocking collectives, shards(): lax.all_to_all(jnp.stack([scaled] * lax.axis_size('snap')), 'snap', 0, 0)  521 us
    reduce_scatter x1, waiting for transfers between devices, shards(): lax.psum_scatter(partial_value, 'space', scatter_dimension=1, tiled=True)  71.9 us
    dot_general x1, matrix products, inner_tile(): lax.dot_general(left, right, (((1,), (1,)), ((), ())), preferred_element_...  13.5 us
  transfers between devices with their start and end apart: 3, of which 3 were waited for; matrix products, arithmetic and copies ran while one was open for 0% of the time, Pallas kernels for 0%

profile of v1, /device:TPU:2, one launch (start us, length us, event | category | flops | bytes accessed | tf_op | source)
XLA Modules:
  0.0 641.9 jit_solution(13279693279802496060)
XLA Ops:
  6.5 0.0 copy-start
  6.5 0.0 reduce-scatter.2.cloned.1.call-start
  6.5 1.3 fusion.10
  7.8 1.9 collective-permute-start
  9.7 6.0 collective-permute-start.1
  15.8 0.6 cosine_reduce_fusion
  16.4 0.7 fusion.9
  17.9 0.1 sqrt_multiply_fusion
  17.9 0.0 copy-done
  17.9 0.4 fusion.8
  18.3 0.0 copy-start.1
  18.3 0.0 copy-start.2
  18.4 0.7 collective-permute-done
  19.0 1.8 collective-permute-done.1
  20.8 0.3 maximum_convert_fusion
  21.1 0.0 copy-done.1
  21.1 0.0 copy-done.2
  21.2 3.1 fusion.4
  24.2 1.5 copy.4
  25.7 2.6 stack.3
  28.3 521.3 %all_to_all.5 = bf16[16,128,5760]{2,1,0:T(8,128)(2,1)} all-to-all(bf16[16,128,5760]{2,1,0:T(8,128)(2,1)S(1)} %stack.3), channel_id=1, replica_groups=mesh['snap'=16,'space'=16] {'snap'}, dimensions={0} | all-to-all | bytes 47185920 | tf_op jit(solution)/shard_map/all_to_all | solution.py:50
  549.6 13.5 %fusion.11 = f32[128,2048]{1,0:T(8,128)} fusion(bf16[128,5760]{0,1:T(8,128)(2,1)S(1)} %bitcast.6, bf16[2048,5760]{1,0:T(8,128)(2,1)} %bitcast.4), kind=kOutput, calls=%fused_computation.16 | convolution fusion | flops 3019898880 | bytes 26116096 | tf_op jit(solution)/shard_map/dot_general | solution.py:26
  563.1 0.0 reduce-scatter.2.cloned.1.call-update
  563.1 71.9 %reduce-scatter.2.cloned.1.call-done = f32[128,128]{1,0:T(8,128)} async-done(((f32[128,2048]{1,0:T(8,128)}), f32[128,128]{1,0:T(8,128)}) %reduce-scatter.2.cloned.1.call-update) | async-done | bytes 65552 | tf_op jit(solution)/shard_map/reduce_scatter | solution.py:53
Async XLA Ops:
  6.5 11.4 %copy-start = (bf16[128,2,4,720]{0,3,2,1:T(8,128)(2,1)S(1)}, bf16[128,2,4,720]{0,3,2,1:T(8,128)(2,1)}, u32[]{:S(2)}) copy-start(bf16[128,2,4,720]{0,3,2,1:T(8,128)(2,1)} %param.3) | copy-start | bytes 4423684
  6.5 628.5 %reduce-scatter.2.cloned.1.call-start = ((), (), s32[]{:S(2)}) async-start(), calls=%async_computation.2 | async-start | bytes 1114112 | tf_op jit(solution)/shard_map/reduce_scatter | solution.py:53
  7.8 11.2 %collective-permute-start = (bf16[128,2,1,720]{0,3,2,1:T(8,128)(2,1)S(1)}, bf16[128,2,1,720]{0,3,2,1:T(8,128)(2,1)S(1)}, u32[]{:S(2)}, u32[]{:S(2)}) collective-permute-start(bf16[128,2,1,720]{0,3,2,1:T(8,128)(2,1)S(1)} %get-tuple-element.9), channel_id=1, source_target_pairs={{0,1},{1,2},{2,3},{3,4},{4,5},{5,6},{6,7},{7,8},{8,9},{9,10},{10,1... | collective-permute-start | bytes 1105928 | tf_op jit(solution)/shard_map/ppermute | solution.py:16
  9.7 11.1 %collective-permute-start.1 = (bf16[128,2,1,720]{0,3,2,1:T(8,128)(2,1)S(1)}, bf16[128,2,1,720]{0,3,2,1:T(8,128)(2,1)S(1)}, u32[]{:S(2)}, u32[]{:S(2)}) collective-permute-start(bf16[128,2,1,720]{0,3,2,1:T(8,128)(2,1)S(1)} %get-tuple-element.10), channel_id=1, source_target_pairs={{1,0},{2,1},{3,2},{4,3},{5,4},{6,5},{7,6},{8,7},{9,8},{10,9},{11,1... | collective-permute-start | bytes 1105928 | tf_op jit(solution)/shard_map/ppermute | solution.py:18
  18.3 2.8 copy-start.1
  18.3 2.8 copy-start.2
Sparse Core Ops, SparseCore 0:
  563.2 71.7 reduce-scatter.1
